TPU v7x, 256 devices: a whole 4x4x8 slice. The times are simulated.
256 devices in a mesh: ctx: 8 (over x_hi, y), ep: 32 (over z, x_lo, core).
Axes of the slice: x: 4 (x_hi: 2, x_lo: 2; x = x_hi * 2 + x_lo), y: 4, z: 8, core: 2. Of those that a mesh axis runs over, the one named last changes fastest.
Arguments:
- queries: bfloat16 [32, 1024, 2048], P('ep', 'ctx'), may hold values from -28 to 28
- keys: bfloat16 [32, 1024, 256], P('ep', 'ctx'), may hold values from -6 to 6
- values: bfloat16 [32, 1024, 256], P('ep', 'ctx'), may hold values from -6 to 6
- docs: int32 [32, 1024], P('ep', 'ctx'), may hold values from 0 to 2, as said below
- resid: bfloat16 [32, 1024, 2048], P('ep', 'ctx'), may hold values from -6 to 6
- norm_gain: float32 [2048], replicated, may hold values from 0.25 to 1.75
- routes: int32 [32, 1024, 4], P('ep', 'ctx'), may hold values from 0 to 31, all different within a row; in each aligned block of 128 rows (0 to 127, 128 to 255, ..., all dimensions but the last counted through in order) at most 20 rows name the same one
- gates: float32 [32, 1024, 4], P('ep', 'ctx'), may hold values from 0.1 to 1
- w_gate: bfloat16 [32, 2048, 384], P('ep', 'ctx'), may hold values from -0.125 to 0.125
- w_up: bfloat16 [32, 2048, 384], P('ep', 'ctx'), may hold values from -0.125 to 0.125
- w_down: bfloat16 [32, 2048, 384], P('ep', 'ctx'), may hold values from -0.3125 to 0.3125
- grad_out: bfloat16 [32, 1024, 2048], P('ep', 'ctx'), may hold values from -6 to 6
Outputs:
- block_out: bfloat16 [32, 1024, 2048], P('ep', 'ctx')
- query_grad: bfloat16 [32, 1024, 2048], P('ep', 'ctx')
- key_grad: bfloat16 [32, 1024, 256], P('ep', 'ctx')
- value_grad: bfloat16 [32, 1024, 256], P('ep', 'ctx')
- resid_grad: bfloat16 [32, 1024, 2048], P('ep', 'ctx')
- gate_grad: float32 [32, 1024, 4], P('ep', 'ctx')
- w_gate_grad: bfloat16 [32, 2048, 384], P('ep', 'ctx')
- w_up_grad: bfloat16 [32, 2048, 384], P('ep', 'ctx')
- w_down_grad: bfloat16 [32, 2048, 384], P('ep', 'ctx')
Inputs may be any that keep to these rules, and one draw needn't show every extreme that they name: `docs`: each sequence holds exactly three documents, ids 0, 1 and 2, each a run of one or more positions, in this order. `routes`: the 4 entries of a token name different experts. Among the tokens of one device (the aligned blocks of 128 positions of a sequence), no expert is named more than 20 times, a bound that some block reaches.
All inputs are finite; a program needn't handle non-finite values.
Results may differ from a plain program's by a relative error of at most 0.04.
Values may be sent and summed in bfloat16 or wider, within the bound.
A program may use at most 128 MiB of HBM per device.

v0:
```python
import jax
import jax.numpy as jnp
from jax import lax
from jax.sharding import PartitionSpec as P

HD = 128


def attention_probs(query_rows, key_rows, query_docs, key_docs, query_start):
    count = query_rows.shape[0]
    total = key_rows.shape[0]
    heads_kv = key_rows.shape[1] // HD
    grouped = query_rows.reshape(count, heads_kv, -1, HD)
    keyed = key_rows.reshape(total, heads_kv, HD)
    query_places = query_start + jnp.arange(count)
    key_places = jnp.arange(total)
    allowed = (query_docs[:, None] == key_docs[None, :]) & (
        key_places[None, :] <= query_places[:, None]
    )
    offset = jnp.where(allowed, 0.0, -1e30).astype(jnp.float32)
    scores = (
        jnp.einsum("ikgd,jkd->kgij", grouped, keyed, preferred_element_type=jnp.float32)
        * float(HD) ** (-0.5)
        + offset
    )
    highest = jnp.max(scores, axis=-1, keepdims=True)
    raised = jnp.exp(scores - highest)
    return raised / jnp.sum(raised, axis=-1, keepdims=True)


def route_rows(rows, n_ep):
    return lax.all_to_all(
        rows.reshape(n_ep, -1, rows.shape[-1]), "ep", split_axis=0, concat_axis=0, tiled=True
    )


def per_device(
    queries, keys, values, docs, resid, norm_gain, routes, gates, w_gate, w_up, w_down, grad_out
):
    tok_rows = queries.shape[1]
    width = resid.shape[2]
    n_ep = lax.axis_size("ep")
    exp_dev = w_gate.shape[0]
    hidden_units = w_gate.shape[2]
    top_count = routes.shape[2]
    experts_all = exp_dev * n_ep
    capacity = max(2, (5 * tok_rows * top_count + 4 * experts_all - 1) // (4 * experts_all))
    query_start = lax.axis_index("ctx") * tok_rows
    score_scale = float(HD) ** (-0.5)
    query_rows = queries[0]
    query_docs = docs[0]
    all_keys, all_values, all_docs = (
        lax.all_gather(keys[0], "ctx", axis=0, tiled=True),
        lax.all_gather(values[0], "ctx", axis=0, tiled=True),
        lax.all_gather(docs[0], "ctx", axis=0, tiled=True),
    )
    total = all_keys.shape[0]
    heads_kv = all_keys.shape[1] // HD
    probs = attention_probs(query_rows, all_keys, query_docs, all_docs, query_start)
    probs_b = probs.astype(jnp.bfloat16)
    value_heads = all_values.reshape(total, heads_kv, HD)
    attn = jnp.einsum("kgij,jkd->ikgd", probs_b, value_heads, preferred_element_type=jnp.float32)
    attn = attn.reshape(tok_rows, width).astype(jnp.bfloat16)
    hidden_f = (
        (resid[0].astype(jnp.float32) + attn.astype(jnp.float32))
        .astype(jnp.bfloat16)
        .astype(jnp.float32)
    )
    rstd = lax.rsqrt(jnp.mean(hidden_f * hidden_f, axis=-1, keepdims=True) + 1e-06)
    normed = (hidden_f * rstd * norm_gain).astype(jnp.bfloat16)
    flat_routes = routes[0].reshape(tok_rows * top_count)
    onehot = (flat_routes[:, None] == jnp.arange(experts_all, dtype=jnp.int32)[None, :]).astype(
        jnp.int32
    )
    ranks = jnp.cumsum(onehot, axis=0) - onehot
    slots = jnp.sum(ranks * onehot, axis=-1)
    targets = flat_routes * capacity + slots
    repeated = jnp.repeat(normed, top_count, axis=0)
    outgoing = jnp.zeros((experts_all * capacity, width), jnp.bfloat16).at[targets].set(repeated)
    upstream = grad_out[0]
    upstream_rep = jnp.repeat(upstream, top_count, axis=0).astype(jnp.float32)
    gate_flat = gates[0].reshape(tok_rows * top_count)
    d_out_rows = (gate_flat[:, None] * upstream_rep).astype(jnp.bfloat16)
    outgoing_grad = (
        jnp.zeros((experts_all * capacity, width), jnp.bfloat16).at[targets].set(d_out_rows)
    )
    received = route_rows(outgoing, n_ep).reshape(n_ep, exp_dev, capacity, width)
    gate_full, up_full, down_full = (
        lax.all_gather(w_gate, "ctx", axis=1, tiled=True),
        lax.all_gather(w_up, "ctx", axis=1, tiled=True),
        lax.all_gather(w_down, "ctx", axis=1, tiled=True),
    )
    pre_gate = jnp.einsum("slcd,ldf->slcf", received, gate_full, preferred_element_type=jnp.float32)
    pre_up = jnp.einsum("slcd,ldf->slcf", received, up_full, preferred_element_type=jnp.float32)
    sigma = jax.nn.sigmoid(pre_gate)
    silu_val = pre_gate * sigma
    activ = (silu_val * pre_up).astype(jnp.bfloat16)
    expert_out = jnp.einsum(
        "slcf,ldf->slcd", activ, down_full, preferred_element_type=jnp.float32
    ).astype(jnp.bfloat16)
    returned = route_rows(expert_out, n_ep).reshape(experts_all * capacity, width)
    d_out = route_rows(outgoing_grad, n_ep).reshape(n_ep, exp_dev, capacity, width)
    d_activ = jnp.einsum("slcd,ldf->slcf", d_out, down_full, preferred_element_type=jnp.float32)
    d_gate = (d_activ * pre_up * sigma * (1.0 + pre_gate * (1.0 - sigma))).astype(jnp.bfloat16)
    d_up = (d_activ * silu_val).astype(jnp.bfloat16)
    d_row = (
        jnp.einsum("slcf,ldf->slcd", d_gate, gate_full, preferred_element_type=jnp.float32)
        + jnp.einsum("slcf,ldf->slcd", d_up, up_full, preferred_element_type=jnp.float32)
    ).astype(jnp.bfloat16)
    shard_rows = w_gate.shape[1]
    gate_term = jnp.einsum("slcd,slcf->dlf", received, d_gate, preferred_element_type=jnp.float32)
    up_term = jnp.einsum("slcd,slcf->dlf", received, d_up, preferred_element_type=jnp.float32)
    down_term = jnp.einsum("slcd,slcf->dlf", d_out, activ, preferred_element_type=jnp.float32)
    summed = lax.psum_scatter(
        jnp.stack([gate_term, up_term, down_term], axis=1)
        .reshape(shard_rows * lax.axis_size("ctx"), 3 * exp_dev * hidden_units)
        .astype(jnp.bfloat16),
        "ctx",
        scatter_dimension=0,
        tiled=True,
    ).astype(jnp.float32)
    summed = (
        summed.reshape(shard_rows, 3, exp_dev, hidden_units)
        .transpose(1, 2, 0, 3)
        .astype(jnp.bfloat16)
    )
    back_rows = route_rows(d_row, n_ep).reshape(experts_all * capacity, width)
    own_out = returned[targets].astype(jnp.float32)
    moe_sum = jnp.sum((gate_flat[:, None] * own_out).reshape(tok_rows, top_count, width), axis=1)
    block_out = (hidden_f + moe_sum).astype(jnp.bfloat16)
    gate_grad = jnp.sum(upstream_rep * own_out, axis=-1).reshape(tok_rows, top_count)
    d_normed = jnp.sum(
        back_rows[targets].astype(jnp.float32).reshape(tok_rows, top_count, width), axis=1
    )
    scaled = norm_gain * d_normed
    resid_grad = (
        upstream.astype(jnp.float32)
        + rstd * scaled
        - hidden_f * rstd**3 * jnp.mean(scaled * hidden_f, axis=-1, keepdims=True)
    )
    resid_grad = resid_grad.astype(jnp.bfloat16)
    grad_heads = resid_grad.reshape(tok_rows, heads_kv, -1, HD)
    attn_heads = attn.reshape(tok_rows, heads_kv, -1, HD)
    delta = jnp.einsum("ikgd,ikgd->kgi", grad_heads, attn_heads, preferred_element_type=jnp.float32)
    d_probs = jnp.einsum(
        "ikgd,jkd->kgij", grad_heads, value_heads, preferred_element_type=jnp.float32
    )
    d_scores = (probs * (d_probs - delta[..., None])).astype(jnp.bfloat16)
    key_heads = all_keys.reshape(total, heads_kv, HD)
    query_heads = query_rows.reshape(tok_rows, heads_kv, -1, HD)
    query_grad = (
        jnp.einsum("kgij,jkd->ikgd", d_scores, key_heads, preferred_element_type=jnp.float32)
        * score_scale
    )
    query_grad = query_grad.reshape(tok_rows, width).astype(jnp.bfloat16)
    key_terms = (
        jnp.einsum("kgij,ikgd->jkd", d_scores, query_heads, preferred_element_type=jnp.float32)
        * score_scale
    )
    value_terms = jnp.einsum(
        "kgij,ikgd->jkd", probs_b, grad_heads, preferred_element_type=jnp.float32
    )
    kv_terms = jnp.concatenate(
        [key_terms.reshape(total, heads_kv * HD), value_terms.reshape(total, heads_kv * HD)], axis=1
    )
    kv_grads = lax.psum_scatter(
        kv_terms.astype(jnp.bfloat16), "ctx", scatter_dimension=0, tiled=True
    ).astype(jnp.float32)
    key_grad = kv_grads[:, : heads_kv * HD].astype(jnp.bfloat16)
    value_grad = kv_grads[:, heads_kv * HD :].astype(jnp.bfloat16)
    return (
        block_out[None],
        query_grad[None],
        key_grad[None],
        value_grad[None],
        resid_grad[None],
        gate_grad[None],
        summed[0],
        summed[1],
        summed[2],
    )


def solution(mesh):
    return jax.shard_map(
        per_device,
        mesh=mesh,
        in_specs=(
            P("ep", "ctx", None),
            P("ep", "ctx", None),
            P("ep", "ctx", None),
            P("ep", "ctx"),
            P("ep", "ctx", None),
            P(),
            P("ep", "ctx", None),
            P("ep", "ctx", None),
            P("ep", "ctx", None),
            P("ep", "ctx", None),
            P("ep", "ctx", None),
            P("ep", "ctx", None),
        ),
        out_specs=(
            P("ep", "ctx", None),
            P("ep", "ctx", None),
            P("ep", "ctx", None),
            P("ep", "ctx", None),
            P("ep", "ctx", None),
            P("ep", "ctx", None),
            P("ep", "ctx", None),
            P("ep", "ctx", None),
            P("ep", "ctx", None),
        ),
        check_vma=False,
    )
```

profile of v0, /device:TPU:27, one launch (start us, length us, event | category | flops | bytes accessed | tf_op | source)
XLA Modules:
  0.0 642.7 jit_solution(3165984337473850861)
XLA Ops:
  9.8 25.7 %all-gather = bf16[1,1024,256]{1,2,0:T(8,128)(2,1)S(1)} all-gather(bf16[1,128,256]{1,2,0:T(8,128)(2,1)S(1)} %copy.75), channel_id=2, replica_groups=mesh['ctx'=8,'ep'=32] {'ctx'}, dimensions={1}, use_global_device_ids=true | all-gather | bytes 589824 | tf_op jit(solution)/shard_map/all_gather | solution.py:53
  37.0 14.6 %all-gather.1 = s32[1,1024]{1,0:T(1,128)S(1)} all-gather(s32[1,128]{1,0:T(1,128)} %param.15), channel_id=3, replica_groups=mesh['ctx'=8,'ep'=32] {'ctx'}, dimensions={1}, use_global_device_ids=true | all-gather | bytes 4608 | tf_op jit(solution)/shard_map/all_gather | solution.py:55
  51.6 29.0 %all-gather.2 = bf16[1,1024,256]{2,1,0:T(8,128)(2,1)S(1)} all-gather(bf16[1,128,256]{2,1,0:T(8,128)(2,1)} %param.14), channel_id=4, replica_groups=mesh['ctx'=8,'ep'=32] {'ctx'}, dimensions={1}, use_global_device_ids=true | all-gather | bytes 589824 | tf_op jit(solution)/shard_map/all_gather | solution.py:54
  81.0 4.9 fusion.69
  98.9 5.4 scatter_custom_fusion
  106.8 24.4 %all-to-all-start = ((bf16[32,20,2048]{2,1,0:T(8,128)(2,1)}), bf16[32,20,2048]{2,1,0:T(8,128)(2,1)}, u32[]{:S(2)}, u32[]{:S(2)}) async-start(bf16[32,20,2048]{2,1,0:T(8,128)(2,1)} %reshape.391), calls=%async_computation | async-start | bytes 6291456 | tf_op jit(solution)/shard_map/all_to_all | solution.py:32
  136.0 5.3 convert_element_type.232
  141.5 6.1 scatter_custom_fusion.1
  150.0 53.2 %all-to-all-done = bf16[32,20,2048]{2,1,0:T(8,128)(2,1)} async-done(((bf16[32,20,2048]{2,1,0:T(8,128)(2,1)}), bf16[32,20,2048]{2,1,0:T(8,128)(2,1)}, u32[]{:S(2)}, u32[]{:S(2)}) %all-to-all-start) | async-done | bytes 2621472 | tf_op jit(solution)/shard_map/all_to_all | solution.py:32
  203.2 5.5 all-to-all-start.2
  209.5 5.2 fusion.21
  214.7 57.1 %all-gather.7.cloned.1.call-done = bf16[1,2048,384]{2,1,0:T(8,128)(2,1)} async-done(((bf16[1,256,384]{2,1,0:T(8,128)(2,1)}), bf16[1,2048,384]{2,1,0:T(8,128)(2,1)}) %all-gather.7.cloned.1.call-update) | async-done | bytes 1572880 | tf_op jit(solution)/shard_map/all_gather | solution.py:89
  271.7 5.2 fusion.25
  276.9 51.5 %all-gather.11.cloned.1.call-done = bf16[1,2048,384]{2,1,0:T(8,128)(2,1)} async-done(((bf16[1,256,384]{2,1,0:T(8,128)(2,1)}), bf16[1,2048,384]{2,1,0:T(8,128)(2,1)}) %all-gather.11.cloned.1.call-update) | async-done | bytes 1572880 | tf_op jit(solution)/shard_map/all_gather | solution.py:91
  341.9 10.8 %all-to-all-start.3 = ((bf16[32,20,2048]{2,1,0:T(8,128)(2,1)}), bf16[32,20,2048]{2,1,0:T(8,128)(2,1)}, u32[]{:S(2)}, u32[]{:S(2)}) async-start(bf16[32,20,2048]{2,1,0:T(8,128)(2,1)} %copy.93), calls=%async_computation.3 | async-start | bytes 6291456 | tf_op jit(solution)/shard_map/all_to_all | solution.py:32
  355.2 5.3 fusion.8
  360.5 64.2 %all-to-all-done.3 = bf16[32,20,2048]{2,1,0:T(8,128)(2,1)} async-done(((bf16[32,20,2048]{2,1,0:T(8,128)(2,1)}), bf16[32,20,2048]{2,1,0:T(8,128)(2,1)}, u32[]{:S(2)}, u32[]{:S(2)}) %all-to-all-start.3) | async-done | bytes 2621472 | tf_op jit(solution)/shard_map/all_to_all | solution.py:32
  436.4 4.9 reduce_sum.77
  447.7 4.9 fusion.2
  474.7 6.1 all-to-all-start.1
  486.1 66.5 %all-to-all-done.1 = bf16[32,20,2048]{2,1,0:T(8,128)(2,1)} async-done(((bf16[32,20,2048]{2,1,0:T(8,128)(2,1)}), bf16[32,20,2048]{2,1,0:T(8,128)(2,1)}, u32[]{:S(2)}, u32[]{:S(2)}) %all-to-all-start.1) | async-done | bytes 2621472 | tf_op jit(solution)/shard_map/all_to_all | solution.py:32
  559.8 4.9 reshape.406
  568.3 5.6 multiply_reduce_fusion.1
  576.9 55.2 %reduce-scatter.5.cloned.1.call-done = bf16[256,1152]{0,1:T(8,128)(2,1)} async-done(((bf16[2048,1152]{0,1:T(8,128)(2,1)}), bf16[256,1152]{0,1:T(8,128)(2,1)}) %reduce-scatter.5.cloned.1.call-update) | async-done | bytes 589840 | tf_op jit(solution)/shard_map/reduce_scatter | solution.py:114
  (151 shorter events, 106.6 us)
Async XLA Ops:
  7.2 73.6 %copy-start.31 = (s32[1,128]{1,0:T(1,128)S(1)}, s32[1,128]{1,0:T(1,128)}, u32[]{:S(2)}) copy-start(s32[1,128]{1,0:T(1,128)} %param.15) | copy-start | bytes 1540
  35.5 50.4 %copy-start.16 = (bf16[1,1024,256]{1,2,0:T(8,128)(2,1)}, bf16[1,1024,256]{1,2,0:T(8,128)(2,1)S(1)}, u32[]{:S(2)}) copy-start(bf16[1,1024,256]{1,2,0:T(8,128)(2,1)S(1)} %all-gather) | copy-start | bytes 1572868
  37.0 48.9 %copy-start.18 = (bf16[1,128,2048]{1,2,0:T(8,128)(2,1)}, bf16[1,128,2048]{1,2,0:T(8,128)(2,1)S(1)}, u32[]{:S(2)}) copy-start(bf16[1,128,2048]{1,2,0:T(8,128)(2,1)S(1)} %copy.142) | copy-start | bytes 1572868
  80.8 9.5 %copy-start.20 = (bf16[1,1024,256]{1,2,0:T(8,128)(2,1)}, bf16[1,1024,256]{1,2,0:T(8,128)(2,1)S(1)}, u32[]{:S(2)}) copy-start(bf16[1,1024,256]{1,2,0:T(8,128)(2,1)S(1)} %copy.78) | copy-start | bytes 1572868
  106.8 25.9 %copy-start.8 = (bf16[1,128,2048]{2,1,0:T(8,128)(2,1)S(1)}, bf16[1,128,2048]{2,1,0:T(8,128)(2,1)}, u32[]{:S(2)}) copy-start(bf16[1,128,2048]{2,1,0:T(8,128)(2,1)} %param.23) | copy-start | bytes 1572868
  106.8 96.4 %all-to-all-start = ((bf16[32,20,2048]{2,1,0:T(8,128)(2,1)}), bf16[32,20,2048]{2,1,0:T(8,128)(2,1)}, u32[]{:S(2)}, u32[]{:S(2)}) async-start(bf16[32,20,2048]{2,1,0:T(8,128)(2,1)} %reshape.391), calls=%async_computation | async-start | bytes 6291456 | tf_op jit(solution)/shard_map/all_to_all | solution.py:32
  131.2 78.3 %all-gather.9.cloned.1.call-start = ((), (), s32[]{:S(2)}) async-start(), calls=%async_computation.7 | async-start | bytes 1769472 | tf_op jit(solution)/shard_map/all_gather | solution.py:90
  131.9 139.8 %all-gather.7.cloned.1.call-start = ((), (), s32[]{:S(2)}) async-start(), calls=%async_computation.6 | async-start | bytes 1769472 | tf_op jit(solution)/shard_map/all_gather | solution.py:89
  136.0 5.3 copy-start.30
  203.2 125.2 %all-to-all-start.2 = ((bf16[32,20,2048]{2,1,0:T(8,128)(2,1)}), bf16[32,20,2048]{2,1,0:T(8,128)(2,1)}, u32[]{:S(2)}, u32[]{:S(2)}) async-start(bf16[32,20,2048]{2,1,0:T(8,128)(2,1)} %reshape.397), calls=%async_computation.2 | async-start | bytes 6291456 | tf_op jit(solution)/shard_map/all_to_all | solution.py:32
  208.7 119.7 %all-gather.11.cloned.1.call-start = ((), (), s32[]{:S(2)}) async-start(), calls=%async_computation.8 | async-start | bytes 1769472 | tf_op jit(solution)/shard_map/all_gather | solution.py:91
  341.9 12.2 %copy-start.10 = (bf16[1,128,2048]{2,1,0:T(8,128)(2,1)S(1)}, bf16[1,128,2048]{2,1,0:T(8,128)(2,1)}, u32[]{:S(2)}) copy-start(bf16[1,128,2048]{2,1,0:T(8,128)(2,1)} %param.16) | copy-start | bytes 1572868
  341.9 82.8 %all-to-all-start.3 = ((bf16[32,20,2048]{2,1,0:T(8,128)(2,1)}), bf16[32,20,2048]{2,1,0:T(8,128)(2,1)}, u32[]{:S(2)}, u32[]{:S(2)}) async-start(bf16[32,20,2048]{2,1,0:T(8,128)(2,1)} %copy.93), calls=%async_computation.3 | async-start | bytes 6291456 | tf_op jit(solution)/shard_map/all_to_all | solution.py:32
  352.7 222.8 %reduce-scatter.3.cloned.1.call-start = ((), (), s32[]{:S(2)}) async-start(), calls=%async_computation.9 | async-start | bytes 1179648 | tf_op jit(solution)/shard_map/reduce_scatter | solution.py:166
  436.4 6.2 copy-start.13
  447.7 7.0 %copy-start.19 = (bf16[1,128,2048]{1,2,0:T(8,128)(2,1)S(1)}, bf16[1,128,2048]{1,2,0:T(8,128)(2,1)}, u32[]{:S(2)}) copy-start(bf16[1,128,2048]{1,2,0:T(8,128)(2,1)} %copy-done.18) | copy-start | bytes 1572868
  457.5 174.6 %reduce-scatter.5.cloned.1.call-start = ((), (), s32[]{:S(2)}) async-start(), calls=%async_computation.10 | async-start | bytes 5308416 | tf_op jit(solution)/shard_map/reduce_scatter | solution.py:114
  474.7 6.2 copy-start.7
  474.7 7.5 %copy-start.17 = (bf16[1,1024,256]{1,2,0:T(8,128)(2,1)S(1)}, bf16[1,1024,256]{1,2,0:T(8,128)(2,1)}, u32[]{:S(2)}) copy-start(bf16[1,1024,256]{1,2,0:T(8,128)(2,1)} %copy-done.16) | copy-start | bytes 1572868
  474.7 77.9 %all-to-all-start.1 = ((bf16[32,20,2048]{2,1,0:T(8,128)(2,1)}), bf16[32,20,2048]{2,1,0:T(8,128)(2,1)}, u32[]{:S(2)}, u32[]{:S(2)}) async-start(bf16[32,20,2048]{2,1,0:T(8,128)(2,1)} %copy.89), calls=%async_computation.1 | async-start | bytes 6291456 | tf_op jit(solution)/shard_map/all_to_all | solution.py:32
  559.8 4.9 copy-start.2
  567.5 6.4 copy-start.5
  567.5 6.4 copy-start.11
  567.6 6.4 copy-start.15
  (18 other events, 45.0 us)
Sparse Core Ops, SparseCore 0:
  134.6 67.3 all-gather.8
  204.6 67.0 all-gather.6
  274.3 54.0 all-gather.10
  457.6 75.7 reduce-scatter.2
  537.5 94.6 reduce-scatter.4
where the time goes:
time: 655 us; the launch traced here: 643 us
  waiting for transfers between devices  349 us (53%)
  local copies, waits for them, and re-layouts  73.9 us (11%)
  blocking collectives  69.2 us (11%)
  matrix products  50.5 us (8%)
  starting transfers between devices  47.9 us (7%)
  other arithmetic  37.2 us (6%)
  between operations  14.8 us (2%)
    all_to_all x4, waiting for transfers between devices, route_rows(): lax.all_to_all(rows.reshape(n_ep, -1, rows.shape[-1]), 'ep', split_axis=0...  184 us
    all_gather x1, waiting for transfers between devices, per_device(): lax.all_gather(w_gate, 'ctx', axis=1, tiled=True)  57.1 us
    reduce_scatter x1, waiting for transfers between devices, per_device(): lax.psum_scatter(jnp.stack([gate_term, up_term, down_term], axis=1).resha...  55.2 us
    all_gather x1, waiting for transfers between devices, per_device(): lax.all_gather(w_down, 'ctx', axis=1, tiled=True)  51.5 us
    all_to_all x4, starting transfers between devices, route_rows(): lax.all_to_all(rows.reshape(n_ep, -1, rows.shape[-1]), 'ep', split_axis=0...  46.7 us
    all_gather x1, blocking collectives, per_device(): lax.all_gather(values[0], 'ctx', axis=0, tiled=True)  29 us
    all_gather x1, blocking collectives, per_device(): lax.all_gather(keys[0], 'ctx', axis=0, tiled=True)  25.7 us
    all_gather x1, blocking collectives, per_device(): lax.all_gather(docs[0], 'ctx', axis=0, tiled=True)  14.6 us
  transfers between devices with their start and end apart: 9, of which 6 were waited for; matrix products, arithmetic and copies ran while one was open for 12% of the time, Pallas kernels for 0%

commit v1 on v0

v1 whole, which is shorter than its diff:
```python
import functools

import jax
import jax.numpy as jnp
from jax import lax
from jax.experimental import pallas as pl
from jax.experimental.pallas import tpu as pltpu
from jax.sharding import PartitionSpec as P

HD = 128
NQ = 4
MESH = pl.DeviceIdType.MESH
F32 = jnp.float32
BF16 = jnp.bfloat16


def dot_nn(a, b):
    return lax.dot_general(a, b, (((1,), (0,)), ((), ())), preferred_element_type=F32)


def dot_nt(a, b):
    return lax.dot_general(a, b, (((1,), (1,)), ((), ())), preferred_element_type=F32)


def dot_tn(a, b):
    return lax.dot_general(a, b, (((0,), (0,)), ((), ())), preferred_element_type=F32)


def iota(shape, dim):
    return lax.broadcasted_iota(jnp.int32, shape, dim)


def block_kernel(
    dims,
    q_ref, k_ref, v_ref, docs_ref, resid_ref, gain_ref, routes_ref, gates_ref,
    wg_ref, wu_ref, wd_ref, go_ref,
    bo_ref, qg_ref, kg_ref, vg_ref, rg_ref, gg_ref, wgo_ref, wuo_ref, wdo_ref,
    dsend, drecv, nsend, nrecv, dret, eret, sel, grows, stk, acc, code_t, gate_t, vt,
    kfull, vfull, docsend, docall, offs, probs, attn, wgu, wdn, xall, doall, dact, dab, act,
    unst, wsend, wrecv, dk_t, dv_t, kvsend, kvrecv,
    ds_s, ds_r, ns_s, ns_r, dr_s, dr_r, er_s, er_r, kv_s, kv_r, w_s, w_r, wg_s, wg_r, kg_s, kg_r,
):
    tok, width, n_ep, n_ctx, cap, top, ff, heads_kv = dims
    ep = lax.axis_index("ep")
    ctx = lax.axis_index("ctx")
    qw = width // NQ
    slab = NQ * cap
    rows_all = n_ep * cap
    group_slabs = 4
    per = 2 if n_ep % 8 == 0 and n_ep >= 32 else 1
    chunk_slabs = group_slabs * per
    n_chunks = n_ep // chunk_slabs
    chunk_rows = chunk_slabs * cap
    shard = width // n_ctx
    heads = width // HD
    group = heads // heads_kv
    scale = float(HD) ** (-0.5)
    kd = heads_kv * HD

    def ep_of(p):
        half = (p + 1) // 2
        odd = p % 2
        return (ep + odd * half + (1 - odd) * (n_ep - half)) % n_ep

    def ep_back(p):
        half = (p + 1) // 2
        odd = p % 2
        return (ep + (1 - odd) * half + odd * (n_ep - half)) % n_ep

    def ctx_of(p):
        return (ctx + p) % n_ctx

    def loop(lo, hi, body):
        def step(i, c):
            body(i)
            return c

        lax.fori_loop(lo, hi, step, 0)

    def rows(start, size, mult):
        return pl.ds(pl.multiple_of(start, mult), size)

    def remote(src, dst, send, recv, axis, dest):
        return pltpu.make_async_remote_copy(
            src_ref=src, dst_ref=dst, send_sem=send, recv_sem=recv,
            device_id={axis: dest}, device_id_type=MESH,
        )

    def to_expert(buf, land, send, recv, p):
        return remote(
            buf.at[rows(ep_of(p) * slab, slab, 16)], land.at[rows(p * slab, slab, 16)],
            send.at[p], recv.at[p], "ep", ep_of(p),
        )

    def to_source(buf, land, send, recv, p):
        return remote(
            buf.at[rows(p * slab, slab, 16)], land.at[rows(ep * slab, slab, 16)],
            send.at[p], recv.at[p], "ep", ep_back(p),
        )

    def own_slab(buf, land, recv, outward):
        mine = rows(ep * slab, slab, 16)
        first = pl.ds(0, slab)
        if outward:
            return pltpu.make_async_copy(buf.at[mine], land.at[first], recv.at[0])
        return pltpu.make_async_copy(buf.at[first], land.at[mine], recv.at[0])

    def kv_copies(p):
        mine = rows(ctx * tok, tok, 128)
        return (
            remote(k_ref, kfull.at[mine], kv_s.at[0, p], kv_r.at[0, p], "ctx", ctx_of(p)),
            remote(v_ref, vfull.at[mine], kv_s.at[1, p], kv_r.at[1, p], "ctx", ctx_of(p)),
            remote(docsend, docall.at[ctx], kv_s.at[2, p], kv_r.at[2, p], "ctx", ctx_of(p)),
        )

    def w_copies(p):
        mine = rows(ctx * shard, shard, 16)
        return (
            remote(wg_ref, wgu.at[mine, pl.ds(0, ff)], w_s.at[0, p], w_r.at[0, p], "ctx", ctx_of(p)),
            remote(wu_ref, wgu.at[mine, pl.ds(ff, ff)], w_s.at[1, p], w_r.at[1, p], "ctx", ctx_of(p)),
            remote(wd_ref, wdn.at[mine], w_s.at[2, p], w_r.at[2, p], "ctx", ctx_of(p)),
        )

    def wg_copy(p):
        return remote(
            wsend.at[rows(ctx_of(p) * shard, shard, 16)], wrecv.at[p],
            wg_s.at[p], wg_r.at[p], "ctx", ctx_of(p),
        )

    def kg_copy(p):
        return remote(
            kvsend.at[rows(ctx_of(p) * tok, tok, 16)], kvrecv.at[p],
            kg_s.at[p], kg_r.at[p], "ctx", ctx_of(p),
        )

    barrier = pltpu.get_barrier_semaphore()
    loop(1, n_ctx, lambda p: pl.semaphore_signal(
        barrier, inc=1, device_id={"ctx": ctx_of(p)}, device_id_type=MESH))
    loop(1, n_ep, lambda p: pl.semaphore_signal(
        barrier, inc=1, device_id={"ep": ep_of(p)}, device_id_type=MESH))
    doc_row = jnp.broadcast_to(docs_ref[...], (8, tok))
    docsend[...] = doc_row

    lane = iota((tok, 128), 1)
    named = jnp.zeros((tok, 128), F32)
    weight = jnp.zeros((tok, 128), F32)
    for k in range(top):
        hit = routes_ref[:, k : k + 1] == lane
        named = jnp.where(hit, 1.0, named)
        weight = jnp.where(hit, gates_ref[:, k : k + 1], weight)
    lower = jnp.where(iota((tok, tok), 0) > iota((tok, tok), 1), 1.0, 0.0).astype(BF16)
    rank = dot_nn(lower, named.astype(BF16))
    code_t[...] = jnp.where(named > 0.5, rank, -1.0).T
    gate_t[...] = weight.T

    row_of = iota((slab, tok), 0)
    quarter = sum((row_of >= j * cap).astype(jnp.int32) for j in range(1, NQ))
    place = (row_of - quarter * cap).astype(F32)

    def build(e):
        hit = jnp.broadcast_to(code_t[pl.ds(e, 1), :], (slab, tok)) == place
        for j in range(NQ):
            sel[rows(e * slab, slab, 16), j * tok : (j + 1) * tok] = jnp.where(
                hit & (quarter == j), 1.0, 0.0).astype(BF16)

    loop(0, n_ep, build)
    for j in range(NQ):
        stk[j * tok : (j + 1) * tok, :] = go_ref[:, j * qw : (j + 1) * qw]

    big = 8 * slab
    n_big = n_ep * slab // big

    def gather_into(dst):
        def body(g):
            at = rows(g * big, big, 16)
            dst[at, :] = dot_nn(sel[at, :], stk[...]).astype(BF16)

        loop(0, n_big, body)

    gather_into(grows)

    def weighted(e):
        hit = jnp.broadcast_to(code_t[pl.ds(e, 1), :], (slab, tok)) == place
        gate = jnp.sum(jnp.where(hit, gate_t[pl.ds(e, 1), :], 0.0), axis=1, keepdims=True)
        at = rows(e * slab, slab, 16)
        dsend[at, :] = (gate * grows[at, :].astype(F32)).astype(BF16)

    loop(0, n_ep, weighted)
    pl.semaphore_wait(barrier, n_ep + n_ctx - 2)

    def start_kv(p):
        for c in kv_copies(p):
            c.start()

    def start_w(p):
        for c in w_copies(p):
            c.start()

    loop(1, n_ctx, start_kv)
    own_slab(dsend, drecv, ds_r, True).start()
    loop(1, n_ep, lambda p: to_expert(dsend, drecv, ds_s, ds_r, p).start())
    loop(1, n_ctx, start_w)

    kfull[rows(ctx * tok, tok, 128), :] = k_ref[...]
    vfull[rows(ctx * tok, tok, 128), :] = v_ref[...]
    docall[ctx] = docsend[...]
    mine_w = rows(ctx * shard, shard, 16)
    wgu[mine_w, 0:ff] = wg_ref[...]
    wgu[mine_w, ff : 2 * ff] = wu_ref[...]
    wdn[mine_w, :] = wd_ref[...]
    out_row = iota((NQ * group_slabs * cap, NQ * group_slabs * cap), 0)
    in_row = iota((NQ * group_slabs * cap, NQ * group_slabs * cap), 1)
    block = group_slabs * cap
    o_q = sum((out_row >= j * block).astype(jnp.int32) for j in range(1, NQ))
    rest = out_row - o_q * block
    o_s = sum((rest >= j * cap).astype(jnp.int32) for j in range(1, group_slabs))
    from_row = o_s * slab + o_q * cap + (rest - o_s * cap)
    unst[...] = jnp.where(in_row == from_row, 1.0, 0.0).astype(BF16)

    def wait_kv(p):
        for c in kv_copies(p):
            c.wait_recv()

    loop(1, n_ctx, wait_kv)

    doc_col = jnp.broadcast_to(docs_ref[...], (tok, tok)).astype(F32).T
    q_pos = ctx * tok + iota((tok, tok), 0)
    for b in range(n_ctx):
        same = doc_col == docall[b, 0:1, :].astype(F32)
        ok = same & (b * tok + iota((tok, tok), 1) <= q_pos)
        offs[:, b * tok : (b + 1) * tok] = jnp.where(ok, 0.0, -1e30)

    def attend(h):
        cols = rows(h * HD, HD, 128)
        kv_cols = rows((h // group) * HD, HD, 128)
        s = dot_nt(q_ref[:, cols], kfull[:, kv_cols]) * scale + offs[...]
        raised = jnp.exp(s - jnp.max(s, axis=1, keepdims=True))
        p = (raised / jnp.sum(raised, axis=1, keepdims=True)).astype(BF16)
        probs[h] = p
        attn[:, cols] = dot_nn(p, vfull[:, kv_cols]).astype(BF16)

    loop(0, heads, attend)

    part = 32

    def hidden_of(at):
        both = resid_ref[at, :].astype(F32) + attn[at, :].astype(F32)
        hidden = both.astype(BF16).astype(F32)
        rstd = lax.rsqrt(jnp.mean(hidden * hidden, axis=1, keepdims=True) + 1e-06)
        return hidden, rstd

    def norm_part(i):
        hidden, rstd = hidden_of(rows(i * part, part, part))
        normed = (hidden * rstd * gain_ref[...]).astype(BF16)
        for j in range(NQ):
            stk[rows(j * tok + i * part, part, part), :] = normed[:, j * qw : (j + 1) * qw]

    loop(0, tok // part, norm_part)
    gather_into(nsend)
    own_slab(nsend, nrecv, ns_r, True).start()
    loop(1, n_ep, lambda p: to_expert(nsend, nrecv, ns_s, ns_r, p).start())

    def wait_w(p):
        for c in w_copies(p):
            c.wait_recv()

    loop(1, n_ctx, wait_w)

    def unstack(src, dst, base_slab, base_row):
        for g in range(per):
            y = dot_nn(unst[...], src[rows(base_slab * slab + g * NQ * block, NQ * block, 16), :])
            y = y.astype(BF16)
            for j in range(NQ):
                dst[rows(base_row + g * block, block, 16), j * qw : (j + 1) * qw] = (
                    y[j * block : (j + 1) * block, :])

    def restack(value, dst, base_slab):
        for g in range(per):
            piece = value[g * block : (g + 1) * block, :]
            tall = jnp.concatenate([piece[:, j * qw : (j + 1) * qw] for j in range(NQ)], axis=0)
            dst[rows(base_slab * slab + g * NQ * block, NQ * block, 16), :] = (
                dot_nn(unst[...], tall).astype(BF16))

    def wait_chunk(buf, land, send, recv, c):
        def one(i):
            to_expert(buf, land, send, recv, c * chunk_slabs + i).wait_recv()

        loop(0, chunk_slabs, one)

    def d_chunk(c):
        wait_chunk(dsend, drecv, ds_s, ds_r, c)
        unstack(drecv, doall, c * chunk_slabs, c * chunk_rows)
        at = rows(c * chunk_rows, chunk_rows, 16)
        dact[at, :] = dot_nn(doall[at, :], wdn[...])

    loop(0, n_chunks, d_chunk)

    def n_chunk(c):
        wait_chunk(nsend, nrecv, ns_s, ns_r, c)
        unstack(nrecv, xall, c * chunk_slabs, c * chunk_rows)
        at = rows(c * chunk_rows, chunk_rows, 16)
        pre = dot_nn(xall[at, :], wgu[...])
        a, b = pre[:, :ff], pre[:, ff:]
        sigma = jax.nn.sigmoid(a)
        silu = a * sigma
        d_act = dact[at, :]
        act[at, :] = (silu * b).astype(BF16)
        dab[at, 0:ff] = (d_act * b * sigma * (1.0 + a * (1.0 - sigma))).astype(BF16)
        dab[at, ff : 2 * ff] = (d_act * silu).astype(BF16)
        restack(dot_nt(dab[at, :], wgu[...]).astype(BF16), drecv, c * chunk_slabs)

        def send_back(i):
            p = c * chunk_slabs + i

            @pl.when(p > 0)
            def _():
                to_source(drecv, dret, dr_s, dr_r, p).start()

        loop(0, chunk_slabs, send_back)
        restack(dot_nt(act[at, :], wdn[...]).astype(BF16), nrecv, c * chunk_slabs)

    loop(0, n_chunks, n_chunk)
    own_slab(drecv, dret, dr_r, False).start()
    own_slab(nrecv, eret, er_r, False).start()
    loop(1, n_ep, lambda p: to_source(nrecv, eret, er_s, er_r, p).start())

    def w_grad(p):
        j = ctx_of(p)
        cols = rows(j * shard, shard, 128)
        at = rows(j * shard, shard, 16)
        wsend[at, 0 : 2 * ff] = dot_tn(xall[:, cols], dab[...]).astype(BF16)
        wsend[at, 2 * ff : 3 * ff] = dot_tn(doall[:, cols], act[...]).astype(BF16)

        @pl.when(p < n_ctx)
        def _():
            wg_copy(p).start()

    loop(1, n_ctx + 1, w_grad)

    def wait_back(buf, land, send, recv):
        def one(p):
            dst = land.at[rows(ep_of(p) * slab, slab, 16)]
            src = buf.at[rows(p * slab, slab, 16)]
            remote(src, dst, send.at[p], recv.at[p], "ep", ep_back(p)).wait_recv()

        loop(1, n_ep, one)
        own_slab(buf, land, recv, False).wait()

    def combine(land):
        acc[...] = jnp.zeros_like(acc)

        def body(g):
            at = rows(g * big, big, 16)
            acc[...] += dot_tn(sel[at, :], land[at, :])

        loop(0, n_big, body)

    def summed(i):
        return jnp.concatenate(
            [acc[rows(j * tok + i * part, part, part), :] for j in range(NQ)], axis=1)

    wait_back(drecv, dret, dr_s, dr_r)
    combine(dret)

    def resid_part(i):
        at = rows(i * part, part, part)
        hidden, rstd = hidden_of(at)
        scaled = gain_ref[...] * summed(i)
        tilt = jnp.mean(scaled * hidden, axis=1, keepdims=True)
        grad = go_ref[at, :].astype(F32) + rstd * scaled - hidden * (rstd * rstd * rstd) * tilt
        rg_ref[at, :] = grad.astype(BF16)

    loop(0, tok // part, resid_part)

    dk_t[...] = jnp.zeros_like(dk_t)
    dv_t[...] = jnp.zeros_like(dv_t)

    def attend_back(h):
        cols = rows(h * HD, HD, 128)
        g = h // group
        kv_cols = rows(g * HD, HD, 128)
        up = rg_ref[:, cols]
        p = probs[h]
        delta = jnp.sum(up.astype(F32) * attn[:, cols].astype(F32), axis=1, keepdims=True)
        d_p = dot_nt(up, vfull[:, kv_cols])
        d_s = (p.astype(F32) * (d_p - delta)).astype(BF16)
        qg_ref[:, cols] = (dot_nn(d_s, kfull[:, kv_cols]) * scale).astype(BF16)
        dk_t[g] += dot_tn(q_ref[:, cols], d_s)
        dv_t[g] += dot_tn(up, p)

    loop(0, heads, attend_back)
    for g in range(heads_kv):
        kvsend[:, g * HD : (g + 1) * HD] = (dk_t[g] * scale).T.astype(BF16)
        kvsend[:, kd + g * HD : kd + (g + 1) * HD] = dv_t[g].T.astype(BF16)
    loop(1, n_ctx, lambda p: kg_copy(p).start())

    wait_back(nrecv, eret, er_s, er_r)

    def gate_part(e):
        at = rows(e * slab, slab, 16)
        hit = jnp.broadcast_to(code_t[pl.ds(e, 1), :], (slab, tok)) == place
        gate = jnp.sum(jnp.where(hit, gate_t[pl.ds(e, 1), :], 0.0), axis=1, keepdims=True)
        out = eret[at, :].astype(F32)
        along = jnp.sum(out * grows[at, :].astype(F32), axis=1, keepdims=True)
        vt[pl.ds(e, 1), :] = jnp.sum(jnp.where(hit, along, 0.0), axis=0, keepdims=True)
        eret[at, :] = (gate * out).astype(BF16)

    vt[...] = jnp.zeros_like(vt)
    loop(0, n_ep, gate_part)
    by_token = vt[...].T
    gate_grad = jnp.zeros((tok, 128), F32)
    for k in range(top):
        hit = routes_ref[:, k : k + 1] == lane
        value = jnp.sum(jnp.where(hit, by_token, 0.0), axis=1, keepdims=True)
        gate_grad = jnp.where(lane == k, value, gate_grad)
    gg_ref[...] = gate_grad[:, :top]
    combine(eret)

    def out_part(i):
        at = rows(i * part, part, part)
        hidden = (resid_ref[at, :].astype(F32) + attn[at, :].astype(F32)).astype(BF16)
        bo_ref[at, :] = (hidden.astype(F32) + summed(i)).astype(BF16)

    loop(0, tok // part, out_part)

    loop(1, n_ctx, lambda p: wg_copy(p).wait_recv())

    def w_out(i):
        at = rows(i * part, part, part)
        total = wsend[rows(ctx * shard + i * part, part, part), :].astype(F32)
        for p in range(1, n_ctx):
            total = total + wrecv[p, at, :].astype(F32)
        total = total.astype(BF16)
        wgo_ref[at, :] = total[:, 0:ff]
        wuo_ref[at, :] = total[:, ff : 2 * ff]
        wdo_ref[at, :] = total[:, 2 * ff : 3 * ff]

    loop(0, shard // part, w_out)
    loop(1, n_ctx, lambda p: kg_copy(p).wait_recv())
    total = kvsend[rows(ctx * tok, tok, 16), :].astype(F32)
    for p in range(1, n_ctx):
        total = total + kvrecv[p].astype(F32)
    kg_ref[...] = total[:, :kd].astype(BF16)
    vg_ref[...] = total[:, kd:].astype(BF16)

    def ep_done(p):
        to_expert(dsend, drecv, ds_s, ds_r, p).wait_send()
        to_expert(nsend, nrecv, ns_s, ns_r, p).wait_send()
        to_source(drecv, dret, dr_s, dr_r, p).wait_send()
        to_source(nrecv, eret, er_s, er_r, p).wait_send()

    def ctx_done(p):
        for c in kv_copies(p) + w_copies(p):
            c.wait_send()
        wg_copy(p).wait_send()
        kg_copy(p).wait_send()

    loop(1, n_ep, ep_done)
    loop(1, n_ctx, ctx_done)


def per_device(
    queries, keys, values, docs, resid, norm_gain, routes, gates, w_gate, w_up, w_down, grad_out
):
    tok, width = queries.shape[1], queries.shape[2]
    n_ep, n_ctx = lax.axis_size("ep"), lax.axis_size("ctx")
    shard, ff = w_gate.shape[1], w_gate.shape[2]
    top = routes.shape[2]
    heads_kv = keys.shape[2] // HD
    cap = max(2, (5 * tok * top + 4 * n_ep - 1) // (4 * n_ep))
    dims = (tok, width, n_ep, n_ctx, cap, top, ff, heads_kv)
    qw, slab, heads, kd = width // NQ, NQ * cap, width // HD, heads_kv * HD
    total, rows_all, tall = tok * n_ctx, n_ep * cap, n_ep * NQ * cap
    dma = pltpu.SemaphoreType.DMA
    vmem = pl.BlockSpec(memory_space=pltpu.VMEM)
    wide = pltpu.VMEM((tall, qw), BF16)
    outs = pl.pallas_call(
        functools.partial(block_kernel, dims),
        out_shape=(
            jax.ShapeDtypeStruct((tok, width), BF16),
            jax.ShapeDtypeStruct((tok, width), BF16),
            jax.ShapeDtypeStruct((tok, kd), BF16),
            jax.ShapeDtypeStruct((tok, kd), BF16),
            jax.ShapeDtypeStruct((tok, width), BF16),
            jax.ShapeDtypeStruct((tok, top), F32),
            jax.ShapeDtypeStruct((shard, ff), BF16),
            jax.ShapeDtypeStruct((shard, ff), BF16),
            jax.ShapeDtypeStruct((shard, ff), BF16),
        ),
        in_specs=[vmem] * 12,
        out_specs=[vmem] * 9,
        scratch_shapes=[
            wide, wide, wide, wide, wide, wide,
            pltpu.VMEM((tall, NQ * tok), BF16), wide,
            pltpu.VMEM((NQ * tok, qw), BF16), pltpu.VMEM((NQ * tok, qw), F32),
            pltpu.VMEM((128, tok), F32), pltpu.VMEM((128, tok), F32), pltpu.VMEM((128, tok), F32),
            pltpu.VMEM((total, kd), BF16), pltpu.VMEM((total, kd), BF16),
            pltpu.VMEM((8, tok), jnp.int32), pltpu.VMEM((n_ctx, 8, tok), jnp.int32),
            pltpu.VMEM((tok, total), F32), pltpu.VMEM((heads, tok, total), BF16),
            pltpu.VMEM((tok, width), BF16),
            pltpu.VMEM((width, 2 * ff), BF16), pltpu.VMEM((width, ff), BF16),
            pltpu.VMEM((rows_all, width), BF16), pltpu.VMEM((rows_all, width), BF16),
            pltpu.VMEM((rows_all, ff), F32), pltpu.VMEM((rows_all, 2 * ff), BF16),
            pltpu.VMEM((rows_all, ff), BF16),
            pltpu.VMEM((4 * slab, 4 * slab), BF16),
            pltpu.VMEM((width, 3 * ff), BF16), pltpu.VMEM((n_ctx, shard, 3 * ff), BF16),
            pltpu.VMEM((heads_kv, HD, total), F32), pltpu.VMEM((heads_kv, HD, total), F32),
            pltpu.VMEM((total, 2 * kd), BF16), pltpu.VMEM((n_ctx, tok, 2 * kd), BF16),
            dma((n_ep,)), dma((n_ep,)), dma((n_ep,)), dma((n_ep,)),
            dma((n_ep,)), dma((n_ep,)), dma((n_ep,)), dma((n_ep,)),
            dma((3, n_ctx)), dma((3, n_ctx)), dma((3, n_ctx)), dma((3, n_ctx)),
            dma((n_ctx,)), dma((n_ctx,)), dma((n_ctx,)), dma((n_ctx,)),
        ],
        compiler_params=pltpu.CompilerParams(
            collective_id=0, has_side_effects=True, vmem_limit_bytes=67_000_000
        ),
        name="moe_block",
    )(
        queries[0], keys[0], values[0], docs, resid[0], norm_gain[None], routes[0], gates[0],
        w_gate[0], w_up[0], w_down[0], grad_out[0],
    )
    return tuple(o[None] for o in outs)


def solution(mesh):
    three = P("ep", "ctx", None)
    return jax.shard_map(
        per_device,
        mesh=mesh,
        in_specs=(
            three, three, three, P("ep", "ctx"), three, P(), three, three,
            three, three, three, three,
        ),
        out_specs=(three,) * 9,
        check_vma=False,
    )
```

time: 655 us -> 298 us (0.45); the launches traced: 643 us -> 297 us
  waiting for transfers between devices: 349 us -> 0 us
  Pallas kernels: 0 us -> 285 us
  blocking collectives: 69.2 us -> 0 us
  local copies, waits for them, and re-layouts: 73.9 us -> 11.7 us
  matrix products: 50.5 us -> 0 us
  starting transfers between devices: 47.9 us -> 0 us
  other arithmetic: 37.2 us -> 0 us
  between operations: 14.8 us -> 0.67 us
    pallas_call x0 -> x1, Pallas kernels: none -> 285 us  [per_device(): pl.pallas_call(functools.partial(block_kernel, dims), out_shape=(jax.Shap...]
    all_to_all x4 -> x0, waiting for transfers between devices: 184 us -> none  [route_rows(): lax.all_to_all(rows.reshape(n_ep, -1, rows.shape[-1]), 'ep', split_axis=0...]
    all_gather x3 -> x0, waiting for transfers between devices: 109 us -> none  [the longest x1 57.1 us: per_device(): lax.all_gather(w_gate, 'ctx', axis=1, tiled=True)]
    all_gather x3 -> x0, blocking collectives: 69.2 us -> none  [the longest x1 29 us: per_device(): lax.all_gather(values[0], 'ctx', axis=0, tiled=True)]
    reduce_scatter x2 -> x0, waiting for transfers between devices: 55.2 us -> none  [the longest x1 55.2 us: per_device(): lax.psum_scatter(jnp.stack([gate_term, up_term, down_term], axis=1).resha...]
    all_to_all x4 -> x0, starting transfers between devices: 46.7 us -> none  [route_rows(): lax.all_to_all(rows.reshape(n_ep, -1, rows.shape[-1]), 'ep', split_axis=0...]
    dot_general x14 -> x0, matrix products: 45.6 us -> none  [the longest x1 5.3 us: per_device(): jnp.einsum('slcd,slcf->dlf', received, d_gate, preferred_element_type=jnp...]
    convert_element_type x9 -> x0, local copies, waits for them, and re-layouts: 25.3 us -> none  [the longest x1 5.31 us: per_device(): upstream_rep = jnp.repeat(upstream, top_count, axis=0).astype(jnp.float32)]
  transfers between devices with their start and end apart: 9 -> 0, of which waited for: 6 -> 0; matrix products, arithmetic and copies ran while one was open for 12% -> 0% of each run, Pallas kernels for 0% -> 0%
where the time goes in v1:
time: 298 us; the launch traced here: 297 us
  Pallas kernels  285 us (96%)
  local copies, waits for them, and re-layouts  11.7 us (4%)
    pallas_call x1, Pallas kernels, per_device(): pl.pallas_call(functools.partial(block_kernel, dims), out_shape=(jax.Shap...  285 us
    unnamed x29, local copies, waits for them, and re-layouts  11.7 us

profile of v1, /device:TPU:27, one launch (start us, length us, event | category | flops | bytes accessed | tf_op | source)
XLA Modules:
  0.0 297.3 jit_solution(4398071589198875234)
XLA Ops:
  0.6 0.0 copy-start.7
  0.7 0.7 copy-done.7
  1.3 0.0 copy-start.8
  1.3 0.7 copy.21
  2.1 0.0 copy-done.8
  2.1 0.7 copy.22
  2.8 284.9 %moe_block.1 = (bf16[128,2048]{1,0:T(8,128)(2,1)}, bf16[128,2048]{1,0:T(8,128)(2,1)}, bf16[128,256]{1,0:T(8,128)(2,1)}, bf16[128,256]{1,0:T(8,128)(2,1)}, bf16[1...) custom-call(bf16[128,2048]{1,0:T(8,128)(2,1)} %bitcast.23, ...), custom_call_target="tpu_custom_call" | custom-call | tf_op jit(solution)/shard_map/moe_block/pallas_call | solution.py:477
  287.7 1.5 copy.23
  289.2 0.0 copy-start.1
  289.2 1.9 copy.32
  291.1 0.0 copy-done.1
  291.1 0.8 copy.33
  291.9 0.1 copy-done.6
  292.0 0.6 copy.34
  292.6 0.2 copy-done.5
  292.8 0.6 copy.35
  293.5 0.0 copy-done
  293.5 0.8 copy.36
  294.3 0.3 copy-done.4
  294.6 0.7 copy.37
  295.3 0.3 copy-done.3
  295.6 0.7 copy.38
  296.3 0.3 copy-done.2
  296.6 0.7 copy.39
  (6 shorter events, 0.0 us)
Async XLA Ops:
  0.6 0.7 copy-start.7
  1.3 0.7 copy-start.8
  289.2 1.9 copy-start.1
  291.1 0.9 copy-start.6
  291.1 2.4 copy-start
  292.0 0.9 copy-start.5
  293.5 1.1 copy-start.4
  294.6 1.0 copy-start.3
  295.6 1.0 copy-start.2

commit v2 on v1

--- a/solution.py
+++ b/solution.py
@@ -70,6 +70,13 @@
     def ctx_of(p):
         return (ctx + p) % n_ctx
 
+    n_y = n_ctx // 2
+    half_at, y_at = ctx // n_y, ctx % n_y
+    across = (1 - half_at) * n_y + y_at
+
+    def y_of(p):
+        return half_at * n_y + (y_at + p) % n_y
+
     def loop(lo, hi, body):
         def step(i, c):
             body(i)
@@ -113,18 +120,41 @@
             remote(docsend, docall.at[ctx], kv_s.at[2, p], kv_r.at[2, p], "ctx", ctx_of(p)),
         )
 
-    def w_copies(p):
+    def w_own(slot, dest):
         mine = rows(ctx * shard, shard, 16)
         return (
-            remote(wg_ref, wgu.at[mine, pl.ds(0, ff)], w_s.at[0, p], w_r.at[0, p], "ctx", ctx_of(p)),
-            remote(wu_ref, wgu.at[mine, pl.ds(ff, ff)], w_s.at[1, p], w_r.at[1, p], "ctx", ctx_of(p)),
-            remote(wd_ref, wdn.at[mine], w_s.at[2, p], w_r.at[2, p], "ctx", ctx_of(p)),
-        )
-
-    def wg_copy(p):
+            remote(wg_ref, wgu.at[mine, pl.ds(0, ff)], w_s.at[0, slot], w_r.at[0, slot], "ctx", dest),
+            remote(wu_ref, wgu.at[mine, pl.ds(ff, ff)], w_s.at[1, slot], w_r.at[1, slot], "ctx", dest),
+            remote(wd_ref, wdn.at[mine], w_s.at[2, slot], w_r.at[2, slot], "ctx", dest),
+        )
+
+    def w_across():
+        return w_own(0, across)
+
+    def w_along(p):
+        return w_own(p, y_of(p))
+
+    def w_relay(p):
+        theirs = rows(across * shard, shard, 16)
+        slot = n_y + p
+        gu, dn = wgu.at[theirs], wdn.at[theirs]
+        return (
+            remote(gu, gu, w_s.at[0, slot], w_r.at[0, slot], "ctx", y_of(p)),
+            remote(dn, dn, w_s.at[2, slot], w_r.at[2, slot], "ctx", y_of(p)),
+        )
+
+    def wg_along(p, half):
+        to_row = (half * n_y + (y_at + p) % n_y) * shard
+        slot = 2 * p + half
         return remote(
-            wsend.at[rows(ctx_of(p) * shard, shard, 16)], wrecv.at[p],
-            wg_s.at[p], wg_r.at[p], "ctx", ctx_of(p),
+            wsend.at[rows(to_row, shard, 16)], wrecv.at[slot],
+            wg_s.at[slot], wg_r.at[slot], "ctx", y_of(p),
+        )
+
+    def wg_across():
+        return remote(
+            wsend.at[rows(across * shard, shard, 16)], wrecv.at[0],
+            wg_s.at[0], wg_r.at[0], "ctx", across,
         )
 
     def kg_copy(p):
@@ -167,7 +197,7 @@
     for j in range(NQ):
         stk[j * tok : (j + 1) * tok, :] = go_ref[:, j * qw : (j + 1) * qw]
 
-    big = 8 * slab
+    big = min(8, n_ep) * slab
     n_big = n_ep * slab // big
 
     def gather_into(dst):
@@ -192,14 +222,15 @@
         for c in kv_copies(p):
             c.start()
 
-    def start_w(p):
-        for c in w_copies(p):
+    def start_all(copies):
+        for c in copies:
             c.start()
 
     loop(1, n_ctx, start_kv)
     own_slab(dsend, drecv, ds_r, True).start()
     loop(1, n_ep, lambda p: to_expert(dsend, drecv, ds_s, ds_r, p).start())
-    loop(1, n_ctx, start_w)
+    start_all(w_across())
+    loop(1, n_y, lambda p: start_all(w_along(p)))
 
     kfull[rows(ctx * tok, tok, 128), :] = k_ref[...]
     vfull[rows(ctx * tok, tok, 128), :] = v_ref[...]
@@ -239,7 +270,11 @@
         probs[h] = p
         attn[:, cols] = dot_nn(p, vfull[:, kv_cols]).astype(BF16)
 
-    loop(0, heads, attend)
+    loop(0, heads // 2, attend)
+    for c in w_across():
+        c.wait_recv()
+    loop(1, n_y, lambda p: start_all(w_relay(p)))
+    loop(heads // 2, heads, attend)
 
     part = 32
 
@@ -261,10 +296,10 @@
     loop(1, n_ep, lambda p: to_expert(nsend, nrecv, ns_s, ns_r, p).start())
 
     def wait_w(p):
-        for c in w_copies(p):
+        for c in w_along(p) + w_relay(p):
             c.wait_recv()
 
-    loop(1, n_ctx, wait_w)
+    loop(1, n_y, wait_w)
 
     def unstack(src, dst, base_slab, base_row):
         for g in range(per):
@@ -324,18 +359,19 @@
     own_slab(nrecv, eret, er_r, False).start()
     loop(1, n_ep, lambda p: to_source(nrecv, eret, er_s, er_r, p).start())
 
-    def w_grad(p):
-        j = ctx_of(p)
+    def w_grad(i):
+        p, half = (i + 2) // 2, i % 2
+        j = half * n_y + (y_at + p) % n_y
         cols = rows(j * shard, shard, 128)
         at = rows(j * shard, shard, 16)
         wsend[at, 0 : 2 * ff] = dot_tn(xall[:, cols], dab[...]).astype(BF16)
         wsend[at, 2 * ff : 3 * ff] = dot_tn(doall[:, cols], act[...]).astype(BF16)
 
-        @pl.when(p < n_ctx)
+        @pl.when(p < n_y)
         def _():
-            wg_copy(p).start()
-
-    loop(1, n_ctx + 1, w_grad)
+            wg_along(p, half).start()
+
+    loop(0, n_ctx, w_grad)
 
     def wait_back(buf, land, send, recv):
         def one(p):
@@ -394,6 +430,25 @@
         kvsend[:, kd + g * HD : kd + (g + 1) * HD] = dv_t[g].T.astype(BF16)
     loop(1, n_ctx, lambda p: kg_copy(p).start())
 
+    def wait_wg(p):
+        wg_along(p, 0).wait_recv()
+        wg_along(p, 1).wait_recv()
+
+    loop(1, n_y, wait_wg)
+
+    def y_sum(row, half, at):
+        total = wsend[row, :].astype(F32)
+        for p in range(1, n_y):
+            total = total + wrecv[2 * p + half, at, :].astype(F32)
+        return total
+
+    def w_other(i):
+        row = rows(across * shard + i * part, part, part)
+        wsend[row, :] = y_sum(row, 1 - half_at, rows(i * part, part, part)).astype(BF16)
+
+    loop(0, shard // part, w_other)
+    wg_across().start()
+
     wait_back(nrecv, eret, er_s, er_r)
 
     def gate_part(e):
@@ -423,14 +478,12 @@
 
     loop(0, tok // part, out_part)
 
-    loop(1, n_ctx, lambda p: wg_copy(p).wait_recv())
+    wg_across().wait_recv()
 
     def w_out(i):
         at = rows(i * part, part, part)
-        total = wsend[rows(ctx * shard + i * part, part, part), :].astype(F32)
-        for p in range(1, n_ctx):
-            total = total + wrecv[p, at, :].astype(F32)
-        total = total.astype(BF16)
+        total = y_sum(rows(ctx * shard + i * part, part, part), half_at, at)
+        total = (total + wrecv[0, at, :].astype(F32)).astype(BF16)
         wgo_ref[at, :] = total[:, 0:ff]
         wuo_ref[at, :] = total[:, ff : 2 * ff]
         wdo_ref[at, :] = total[:, 2 * ff : 3 * ff]
@@ -450,13 +503,28 @@
         to_source(nrecv, eret, er_s, er_r, p).wait_send()
 
     def ctx_done(p):
-        for c in kv_copies(p) + w_copies(p):
+        for c in kv_copies(p):
             c.wait_send()
-        wg_copy(p).wait_send()
         kg_copy(p).wait_send()
+
+    def y_done(p):
+        for c in w_along(p) + w_relay(p):
+            c.wait_send()
+        wg_along(p, 0).wait_send()
+        wg_along(p, 1).wait_send()
 
     loop(1, n_ep, ep_done)
     loop(1, n_ctx, ctx_done)
+    loop(1, n_y, y_done)
+    for c in w_across():
+        c.wait_send()
+    wg_across().wait_send()
+
+
+def hand_over(*refs):
+    half = len(refs) // 2
+    for src, dst in zip(refs[:half], refs[half:]):
+        dst[...] = src[...]
 
 
 def per_device(
@@ -519,6 +587,13 @@
         queries[0], keys[0], values[0], docs, resid[0], norm_gain[None], routes[0], gates[0],
         w_gate[0], w_up[0], w_down[0], grad_out[0],
     )
+    outs = pl.pallas_call(
+        hand_over,
+        out_shape=tuple(jax.ShapeDtypeStruct(o.shape, o.dtype) for o in outs),
+        in_specs=[vmem] * len(outs),
+        out_specs=[vmem] * len(outs),
+        name="outputs",
+    )(*outs)
     return tuple(o[None] for o in outs)
 
 

time: 298 us -> 272 us (0.913)
  Pallas kernels: 285 us -> 267 us
  local copies, waits for them, and re-layouts: 11.7 us -> 3.65 us
    pallas_call x1, Pallas kernels: 285 us -> 264 us  [per_device(): pl.pallas_call(functools.partial(block_kernel, dims), out_shape=(jax.Shap...]
    unnamed x29 -> x7, local copies, waits for them, and re-layouts: 11.7 us -> 3.65 us
    pallas_call x0 -> x1, Pallas kernels: none -> 3.05 us  [per_device(): pl.pallas_call(hand_over, out_shape=tuple((jax.ShapeDtypeStruct(o.shape,...]
where the time goes in v2:
time: 272 us; the launch traced here: 271 us
  Pallas kernels  267 us (98%)
  local copies, waits for them, and re-layouts  3.65 us (1%)
    pallas_call x1, Pallas kernels, per_device(): pl.pallas_call(functools.partial(block_kernel, dims), out_shape=(jax.Shap...  264 us

profile of v2, /device:TPU:27, one launch (start us, length us, event | category | flops | bytes accessed | tf_op | source)
XLA Modules:
  0.0 271.5 jit_solution(16695611583706775963)
XLA Ops:
  0.6 0.0 copy-start
  0.7 0.7 copy-done
  1.3 0.0 copy-start.1
  1.3 0.7 copy.21
  2.1 0.0 copy-done.1
  2.1 0.7 copy.22
  2.8 264.1 %moe_block.1 = (bf16[128,2048]{1,0:T(8,128)(2,1)}, bf16[128,2048]{1,0:T(8,128)(2,1)}, bf16[128,256]{1,0:T(8,128)(2,1)}, bf16[128,256]{1,0:T(8,128)(2,1)}, bf16[1...) custom-call(bf16[128,2048]{1,0:T(8,128)(2,1)} %bitcast.20, ...), custom_call_target="tpu_custom_call" | custom-call | tf_op jit(solution)/shard_map/moe_block/pallas_call | solution.py:545
  266.9 3.0 %outputs.1 = (bf16[128,2048]{1,0:T(8,128)(2,1)}, bf16[128,2048]{1,0:T(8,128)(2,1)}, bf16[128,256]{1,0:T(8,128)(2,1)}, bf16[128,256]{1,0:T(8,128)(2,1)}, bf16[128...) custom-call(bf16[128,2048]{1,0:T(8,128)(2,1)} %get-tuple-element.27., ...), custom_call_target="tpu_custom_call" | custom-call | tf_op jit(solution)/shard_map/outputs/pallas_call | solution.py:590
  270.0 1.5 copy.23
Async XLA Ops:
  0.6 0.7 copy-start
  1.3 0.7 copy-start.1

commit v3 on v2

--- a/solution.py
+++ b/solution.py
@@ -8,6 +8,7 @@
 from jax.sharding import PartitionSpec as P
 
 HD = 128
+PLANE = 4
 NQ = 4
 MESH = pl.DeviceIdType.MESH
 F32 = jnp.float32
@@ -35,10 +36,10 @@
     q_ref, k_ref, v_ref, docs_ref, resid_ref, gain_ref, routes_ref, gates_ref,
     wg_ref, wu_ref, wd_ref, go_ref,
     bo_ref, qg_ref, kg_ref, vg_ref, rg_ref, gg_ref, wgo_ref, wuo_ref, wdo_ref,
-    dsend, drecv, nsend, nrecv, dret, eret, sel, grows, stk, acc, code_t, gate_t, vt,
+    psend, drecv, nrecv, dret, eret, sel, psel, gall, nall, acc, tabs, code_t, gate_t, vt,
     kfull, vfull, docsend, docall, offs, probs, attn, wgu, wdn, xall, doall, dact, dab, act,
     unst, wsend, wrecv, dk_t, dv_t, kvsend, kvrecv,
-    ds_s, ds_r, ns_s, ns_r, dr_s, dr_r, er_s, er_r, kv_s, kv_r, w_s, w_r, wg_s, wg_r, kg_s, kg_r,
+    zg_s, zg_r, zn_s, zn_r, pd_s, pd_r, pn_s, pn_r, dr_s, dr_r, er_s, er_r, kv_s, kv_r, w_s, w_r, wg_s, wg_r, kg_s, kg_r,
 ):
     tok, width, n_ep, n_ctx, cap, top, ff, heads_kv = dims
     ep = lax.axis_index("ep")
@@ -57,15 +58,24 @@
     scale = float(HD) ** (-0.5)
     kd = heads_kv * HD
 
-    def ep_of(p):
+    n_z = n_ep // PLANE
+    z_at, m_at = ep // PLANE, ep % PLANE
+    hops = n_z // 2
+    tall_tok = NQ * tok
+
+    def away(p):
         half = (p + 1) // 2
         odd = p % 2
-        return (ep + odd * half + (1 - odd) * (n_ep - half)) % n_ep
-
-    def ep_back(p):
-        half = (p + 1) // 2
-        odd = p % 2
-        return (ep + (1 - odd) * half + odd * (n_ep - half)) % n_ep
+        return odd * half + (1 - odd) * (n_z - half)
+
+    def z_of(p):
+        return (z_at + away(p)) % n_z
+
+    def z_back(p):
+        return (z_at + n_z - away(p)) % n_z
+
+    def ep_of(p):
+        return (ep + p) % n_ep
 
     def ctx_of(p):
         return (ctx + p) % n_ctx
@@ -93,24 +103,44 @@
             device_id={axis: dest}, device_id_type=MESH,
         )
 
-    def to_expert(buf, land, send, recv, p):
+    def ring(buf, send, recv, step, with_tabs):
+        up, down = (z_at + 1) % n_z, (z_at + n_z - 1) % n_z
+        up_shard, down_shard = (z_at + n_z - step + 1) % n_z, (z_at + step - 1) % n_z
+        last = step == hops
+        size = tall_tok // 2 if last else tall_tok
+        up_rows = rows(up_shard * tall_tok, size, 16)
+        down_rows = rows(down_shard * tall_tok + (tall_tok - size), size, 16)
+        copies = [
+            remote(buf.at[up_rows], buf.at[up_rows], send.at[0, step], recv.at[0, step],
+                   "ep", up * PLANE + m_at),
+            remote(buf.at[down_rows], buf.at[down_rows], send.at[1, step], recv.at[1, step],
+                   "ep", down * PLANE + m_at),
+        ]
+        if with_tabs:
+            copies.append(remote(tabs.at[up_shard], tabs.at[up_shard], send.at[2, step],
+                                 recv.at[2, step], "ep", up * PLANE + m_at))
+            if not last:
+                copies.append(remote(tabs.at[down_shard], tabs.at[down_shard], send.at[3, step],
+                                     recv.at[3, step], "ep", down * PLANE + m_at))
+        return copies
+
+    def plane_copy(land, send, recv, p, j):
+        at = rows((p * PLANE + j) * slab, slab, 16)
+        i = p * PLANE + j
+        return remote(psend.at[at], land.at[at], send.at[i], recv.at[i], "ep",
+                      z_at * PLANE + (m_at + j) % PLANE)
+
+    def to_source(buf, land, send, recv, i):
+        p, j = i // PLANE, i % PLANE
+        dest = z_of(p) * PLANE + (m_at + PLANE - j) % PLANE
         return remote(
-            buf.at[rows(ep_of(p) * slab, slab, 16)], land.at[rows(p * slab, slab, 16)],
-            send.at[p], recv.at[p], "ep", ep_of(p),
+            buf.at[rows(i * slab, slab, 16)], land.at[rows(ep * slab, slab, 16)],
+            send.at[i], recv.at[i], "ep", dest,
         )
 
-    def to_source(buf, land, send, recv, p):
-        return remote(
-            buf.at[rows(p * slab, slab, 16)], land.at[rows(ep * slab, slab, 16)],
-            send.at[p], recv.at[p], "ep", ep_back(p),
-        )
-
-    def own_slab(buf, land, recv, outward):
+    def own_slab(buf, land, recv):
         mine = rows(ep * slab, slab, 16)
-        first = pl.ds(0, slab)
-        if outward:
-            return pltpu.make_async_copy(buf.at[mine], land.at[first], recv.at[0])
-        return pltpu.make_async_copy(buf.at[first], land.at[mine], recv.at[0])
+        return pltpu.make_async_copy(buf.at[pl.ds(0, slab)], land.at[mine], recv.at[0])
 
     def kv_copies(p):
         mine = rows(ctx * tok, tok, 128)
@@ -182,6 +212,35 @@
     rank = dot_nn(lower, named.astype(BF16))
     code_t[...] = jnp.where(named > 0.5, rank, -1.0).T
     gate_t[...] = weight.T
+    tabs[z_at, 0] = code_t[0:n_ep, :]
+    tabs[z_at, 1] = gate_t[0:n_ep, :]
+    own_rows = z_at * tall_tok
+    for j in range(NQ):
+        gall[rows(own_rows + j * tok, tok, 16), :] = go_ref[:, j * qw : (j + 1) * qw]
+    pl.semaphore_wait(barrier, n_ep + n_ctx - 2)
+
+    def start_kv(p):
+        for c in kv_copies(p):
+            c.start()
+
+    def start_all(copies):
+        for c in copies:
+            c.start()
+
+    def wait_all(copies):
+        for c in copies:
+            c.wait_recv()
+
+    def grad_ring(step):
+        return ring(gall, zg_s, zg_r, step, True)
+
+    def norm_ring(step):
+        return ring(nall, zn_s, zn_r, step, False)
+
+    loop(1, n_ctx, start_kv)
+    start_all(grad_ring(1))
+    start_all(w_across())
+    loop(1, n_y, lambda p: start_all(w_along(p)))
 
     row_of = iota((slab, tok), 0)
     quarter = sum((row_of >= j * cap).astype(jnp.int32) for j in range(1, NQ))
@@ -194,43 +253,38 @@
                 hit & (quarter == j), 1.0, 0.0).astype(BF16)
 
     loop(0, n_ep, build)
-    for j in range(NQ):
-        stk[j * tok : (j + 1) * tok, :] = go_ref[:, j * qw : (j + 1) * qw]
-
     big = min(8, n_ep) * slab
     n_big = n_ep * slab // big
 
-    def gather_into(dst):
-        def body(g):
-            at = rows(g * big, big, 16)
-            dst[at, :] = dot_nn(sel[at, :], stk[...]).astype(BF16)
-
-        loop(0, n_big, body)
-
-    gather_into(grows)
-
-    def weighted(e):
-        hit = jnp.broadcast_to(code_t[pl.ds(e, 1), :], (slab, tok)) == place
-        gate = jnp.sum(jnp.where(hit, gate_t[pl.ds(e, 1), :], 0.0), axis=1, keepdims=True)
-        at = rows(e * slab, slab, 16)
-        dsend[at, :] = (gate * grows[at, :].astype(F32)).astype(BF16)
-
-    loop(0, n_ep, weighted)
-    pl.semaphore_wait(barrier, n_ep + n_ctx - 2)
-
-    def start_kv(p):
-        for c in kv_copies(p):
-            c.start()
-
-    def start_all(copies):
-        for c in copies:
-            c.start()
-
-    loop(1, n_ctx, start_kv)
-    own_slab(dsend, drecv, ds_r, True).start()
-    loop(1, n_ep, lambda p: to_expert(dsend, drecv, ds_s, ds_r, p).start())
-    start_all(w_across())
-    loop(1, n_y, lambda p: start_all(w_along(p)))
+    def pack(p, buf, land, send, recv, weighted):
+        zs = z_of(p)
+        gates_of = []
+        for j in range(PLANE):
+            e = z_at * PLANE + (m_at + j) % PLANE
+            hit = jnp.broadcast_to(tabs[zs, 0, pl.ds(e, 1), :], (slab, tok)) == place
+            for k in range(NQ):
+                psel[j * slab : (j + 1) * slab, k * tok : (k + 1) * tok] = jnp.where(
+                    hit & (quarter == k), 1.0, 0.0).astype(BF16)
+            if weighted:
+                gates_of.append(jnp.sum(
+                    jnp.where(hit, tabs[zs, 1, pl.ds(e, 1), :], 0.0), axis=1, keepdims=True))
+        y = dot_nn(psel[...], buf[rows(zs * tall_tok, tall_tok, 16), :])
+        for j in range(PLANE):
+            piece = y[j * slab : (j + 1) * slab, :]
+            if weighted:
+                piece = piece * gates_of[j]
+            to = land if j == 0 else psend
+            to[rows((p * PLANE + j) * slab, slab, 16), :] = piece.astype(BF16)
+        for j in range(1, PLANE):
+            plane_copy(land, send, recv, p, j).start()
+
+    def pack_d(p):
+        pack(p, gall, drecv, pd_s, pd_r, True)
+
+    def pack_n(p):
+        for j in range(1, PLANE):
+            plane_copy(drecv, pd_s, pd_r, p, j).wait_send()
+        pack(p, nall, nrecv, pn_s, pn_r, False)
 
     kfull[rows(ctx * tok, tok, 128), :] = k_ref[...]
     vfull[rows(ctx * tok, tok, 128), :] = v_ref[...]
@@ -270,11 +324,14 @@
         probs[h] = p
         attn[:, cols] = dot_nn(p, vfull[:, kv_cols]).astype(BF16)
 
-    loop(0, heads // 2, attend)
-    for c in w_across():
-        c.wait_recv()
-    loop(1, n_y, lambda p: start_all(w_relay(p)))
-    loop(heads // 2, heads, attend)
+    for step in range(1, hops + 1):
+        loop(heads * (step - 1) // hops, heads * step // hops, attend)
+        if step < hops:
+            wait_all(grad_ring(step))
+            start_all(grad_ring(step + 1))
+        if step == (hops + 1) // 2:
+            wait_all(w_across())
+            loop(1, n_y, lambda p: start_all(w_relay(p)))
 
     part = 32
 
@@ -288,18 +345,15 @@
         hidden, rstd = hidden_of(rows(i * part, part, part))
         normed = (hidden * rstd * gain_ref[...]).astype(BF16)
         for j in range(NQ):
-            stk[rows(j * tok + i * part, part, part), :] = normed[:, j * qw : (j + 1) * qw]
+            nall[rows(own_rows + j * tok + i * part, part, part), :] = (
+                normed[:, j * qw : (j + 1) * qw])
 
     loop(0, tok // part, norm_part)
-    gather_into(nsend)
-    own_slab(nsend, nrecv, ns_r, True).start()
-    loop(1, n_ep, lambda p: to_expert(nsend, nrecv, ns_s, ns_r, p).start())
+    start_all(norm_ring(1))
 
     def wait_w(p):
         for c in w_along(p) + w_relay(p):
             c.wait_recv()
-
-    loop(1, n_y, wait_w)
 
     def unstack(src, dst, base_slab, base_row):
         for g in range(per):
@@ -316,22 +370,19 @@
             dst[rows(base_slab * slab + g * NQ * block, NQ * block, 16), :] = (
                 dot_nn(unst[...], tall).astype(BF16))
 
-    def wait_chunk(buf, land, send, recv, c):
-        def one(i):
-            to_expert(buf, land, send, recv, c * chunk_slabs + i).wait_recv()
-
-        loop(0, chunk_slabs, one)
+    def wait_chunk(land, send, recv, c):
+        for i in range(per):
+            for j in range(1, PLANE):
+                plane_copy(land, send, recv, c * per + i, j).wait_recv()
 
     def d_chunk(c):
-        wait_chunk(dsend, drecv, ds_s, ds_r, c)
+        wait_chunk(drecv, pd_s, pd_r, c)
         unstack(drecv, doall, c * chunk_slabs, c * chunk_rows)
         at = rows(c * chunk_rows, chunk_rows, 16)
         dact[at, :] = dot_nn(doall[at, :], wdn[...])
 
-    loop(0, n_chunks, d_chunk)
-
     def n_chunk(c):
-        wait_chunk(nsend, nrecv, ns_s, ns_r, c)
+        wait_chunk(nrecv, pn_s, pn_r, c)
         unstack(nrecv, xall, c * chunk_slabs, c * chunk_rows)
         at = rows(c * chunk_rows, chunk_rows, 16)
         pre = dot_nn(xall[at, :], wgu[...])
@@ -354,9 +405,44 @@
         loop(0, chunk_slabs, send_back)
         restack(dot_nt(act[at, :], wdn[...]).astype(BF16), nrecv, c * chunk_slabs)
 
-    loop(0, n_chunks, n_chunk)
-    own_slab(drecv, dret, dr_r, False).start()
-    own_slab(nrecv, eret, er_r, False).start()
+    def fill(step):
+        if step == 1:
+            loop(0, n_z // 2, pack_d)
+        if step == 2:
+            wait_all(grad_ring(hops))
+            loop(n_z // 2, n_z, pack_d)
+        if step == 3:
+            loop(1, n_y, wait_w)
+            loop(0, n_chunks // 2, d_chunk)
+        if step == 4:
+            loop(n_chunks // 2, n_chunks, d_chunk)
+            if hops >= 4:
+                loop(0, n_chunks // 2, n_chunk)
+
+    packed = 0
+    for step in range(1, max(hops, 4) + 1):
+        if step > hops and packed < n_z:
+            fill(step)
+            continue
+        fill(step)
+        if hops >= 4:
+            wait_all(norm_ring(step))
+            if step < hops:
+                start_all(norm_ring(step + 1))
+            ready = n_z if step == hops else 2 * step + 1
+            if step >= 2:
+                loop(packed, ready, pack_n)
+                packed = ready
+    if hops < 4:
+        for step in range(1, hops + 1):
+            wait_all(norm_ring(step))
+            if step < hops:
+                start_all(norm_ring(step + 1))
+        loop(0, n_z, pack_n)
+        loop(0, n_chunks // 2, n_chunk)
+    loop(n_chunks // 2, n_chunks, n_chunk)
+    own_slab(drecv, dret, dr_r).start()
+    own_slab(nrecv, eret, er_r).start()
     loop(1, n_ep, lambda p: to_source(nrecv, eret, er_s, er_r, p).start())
 
     def w_grad(i):
@@ -374,13 +460,15 @@
     loop(0, n_ctx, w_grad)
 
     def wait_back(buf, land, send, recv):
-        def one(p):
-            dst = land.at[rows(ep_of(p) * slab, slab, 16)]
-            src = buf.at[rows(p * slab, slab, 16)]
-            remote(src, dst, send.at[p], recv.at[p], "ep", ep_back(p)).wait_recv()
+        def one(i):
+            p, j = i // PLANE, i % PLANE
+            frm = z_back(p) * PLANE + (m_at + j) % PLANE
+            dst = land.at[rows(frm * slab, slab, 16)]
+            src = buf.at[rows(i * slab, slab, 16)]
+            remote(src, dst, send.at[i], recv.at[i], "ep", frm).wait_recv()
 
         loop(1, n_ep, one)
-        own_slab(buf, land, recv, False).wait()
+        own_slab(buf, land, recv).wait()
 
     def combine(land):
         acc[...] = jnp.zeros_like(acc)
@@ -395,6 +483,15 @@
         return jnp.concatenate(
             [acc[rows(j * tok + i * part, part, part), :] for j in range(NQ)], axis=1)
 
+    for step in range(1, hops + 1):
+        for c in norm_ring(step):
+            c.wait_send()
+
+    def take_rows(g):
+        at = rows(g * big, big, 16)
+        nall[at, :] = dot_nn(sel[at, :], gall[rows(own_rows, tall_tok, 16), :]).astype(BF16)
+
+    loop(0, n_big, take_rows)
     wait_back(drecv, dret, dr_s, dr_r)
     combine(dret)
 
@@ -456,7 +553,7 @@
         hit = jnp.broadcast_to(code_t[pl.ds(e, 1), :], (slab, tok)) == place
         gate = jnp.sum(jnp.where(hit, gate_t[pl.ds(e, 1), :], 0.0), axis=1, keepdims=True)
         out = eret[at, :].astype(F32)
-        along = jnp.sum(out * grows[at, :].astype(F32), axis=1, keepdims=True)
+        along = jnp.sum(out * nall[at, :].astype(F32), axis=1, keepdims=True)
         vt[pl.ds(e, 1), :] = jnp.sum(jnp.where(hit, along, 0.0), axis=0, keepdims=True)
         eret[at, :] = (gate * out).astype(BF16)
 
@@ -496,11 +593,18 @@
     kg_ref[...] = total[:, :kd].astype(BF16)
     vg_ref[...] = total[:, kd:].astype(BF16)
 
-    def ep_done(p):
-        to_expert(dsend, drecv, ds_s, ds_r, p).wait_send()
-        to_expert(nsend, nrecv, ns_s, ns_r, p).wait_send()
-        to_source(drecv, dret, dr_s, dr_r, p).wait_send()
-        to_source(nrecv, eret, er_s, er_r, p).wait_send()
+    def ep_done(i):
+        to_source(drecv, dret, dr_s, dr_r, i).wait_send()
+        to_source(nrecv, eret, er_s, er_r, i).wait_send()
+
+    def plane_done(p):
+        for j in range(1, PLANE):
+            plane_copy(nrecv, pn_s, pn_r, p, j).wait_send()
+
+    loop(0, n_z, plane_done)
+    for step in range(1, hops + 1):
+        for c in grad_ring(step):
+            c.wait_send()
 
     def ctx_done(p):
         for c in kv_copies(p):
@@ -540,6 +644,8 @@
     qw, slab, heads, kd = width // NQ, NQ * cap, width // HD, heads_kv * HD
     total, rows_all, tall = tok * n_ctx, n_ep * cap, n_ep * NQ * cap
     dma = pltpu.SemaphoreType.DMA
+    n_z = n_ep // PLANE
+    ring = n_z // 2 + 1
     vmem = pl.BlockSpec(memory_space=pltpu.VMEM)
     wide = pltpu.VMEM((tall, qw), BF16)
     outs = pl.pallas_call(
@@ -558,9 +664,11 @@
         in_specs=[vmem] * 12,
         out_specs=[vmem] * 9,
         scratch_shapes=[
-            wide, wide, wide, wide, wide, wide,
-            pltpu.VMEM((tall, NQ * tok), BF16), wide,
-            pltpu.VMEM((NQ * tok, qw), BF16), pltpu.VMEM((NQ * tok, qw), F32),
+            wide, wide, wide, wide, wide,
+            pltpu.VMEM((tall, NQ * tok), BF16), pltpu.VMEM((PLANE * slab, NQ * tok), BF16),
+            pltpu.VMEM((n_z * NQ * tok, qw), BF16),
+            pltpu.VMEM((max(n_z * NQ * tok, tall), qw), BF16),
+            pltpu.VMEM((NQ * tok, qw), F32), pltpu.VMEM((n_z, 2, n_ep, tok), F32),
             pltpu.VMEM((128, tok), F32), pltpu.VMEM((128, tok), F32), pltpu.VMEM((128, tok), F32),
             pltpu.VMEM((total, kd), BF16), pltpu.VMEM((total, kd), BF16),
             pltpu.VMEM((8, tok), jnp.int32), pltpu.VMEM((n_ctx, 8, tok), jnp.int32),
@@ -574,6 +682,7 @@
             pltpu.VMEM((width, 3 * ff), BF16), pltpu.VMEM((n_ctx, shard, 3 * ff), BF16),
             pltpu.VMEM((heads_kv, HD, total), F32), pltpu.VMEM((heads_kv, HD, total), F32),
             pltpu.VMEM((total, 2 * kd), BF16), pltpu.VMEM((n_ctx, tok, 2 * kd), BF16),
+            dma((4, ring)), dma((4, ring)), dma((2, ring)), dma((2, ring)),
             dma((n_ep,)), dma((n_ep,)), dma((n_ep,)), dma((n_ep,)),
             dma((n_ep,)), dma((n_ep,)), dma((n_ep,)), dma((n_ep,)),
             dma((3, n_ctx)), dma((3, n_ctx)), dma((3, n_ctx)), dma((3, n_ctx)),

time: 272 us -> 254 us (0.934)
  the two profiles are of different devices: /device:TPU:27 before, /device:TPU:248 now
where the time goes in v3:
time: 254 us
  Pallas kernels  249 us (98%)
  local copies, waits for them, and re-layouts  3.65 us (1%)
    pallas_call x1, Pallas kernels, per_device(): pl.pallas_call(functools.partial(block_kernel, dims), out_shape=(jax.Shap...  246 us

profile of v3, /device:TPU:248, one launch (start us, length us, event | category | flops | bytes accessed | tf_op | source)
XLA Modules:
  0.0 253.8 jit_solution(9941799483940107862)
XLA Ops:
  0.6 0.0 copy-start
  0.7 0.7 copy-done
  1.3 0.0 copy-start.1
  1.3 0.7 copy.21
  2.1 0.0 copy-done.1
  2.1 0.7 copy.22
  2.8 246.4 %moe_block.1 = (bf16[128,2048]{1,0:T(8,128)(2,1)}, bf16[128,2048]{1,0:T(8,128)(2,1)}, bf16[128,256]{1,0:T(8,128)(2,1)}, bf16[128,256]{1,0:T(8,128)(2,1)}, bf16[1...) custom-call(bf16[128,2048]{1,0:T(8,128)(2,1)} %bitcast.20, ...), custom_call_target="tpu_custom_call" | custom-call | tf_op jit(solution)/shard_map/moe_block/pallas_call | solution.py:651
  249.2 3.0 %outputs.1 = (bf16[128,2048]{1,0:T(8,128)(2,1)}, bf16[128,2048]{1,0:T(8,128)(2,1)}, bf16[128,256]{1,0:T(8,128)(2,1)}, bf16[128,256]{1,0:T(8,128)(2,1)}, bf16[128...) custom-call(bf16[128,2048]{1,0:T(8,128)(2,1)} %get-tuple-element.27., ...), custom_call_target="tpu_custom_call" | custom-call | tf_op jit(solution)/shard_map/outputs/pallas_call | solution.py:699
  252.3 1.5 copy.23
Async XLA Ops:
  0.6 0.7 copy-start
  1.3 0.7 copy-start.1
